TPU v7x, 32 devices: a whole 2x2x4 slice. The times are simulated.
32 devices in a mesh: space: 16 (over z, x, core), mode: 2 (over y).
Axes of the slice: x: 2, y: 2, z: 4, core: 2. Of those that a mesh axis runs over, the one named last changes fastest.
Arguments:
- field: float32 [3, 16, 128, 64, 256], P(None, 'mode', 'space'), may hold values from -6 to 6
- velocity: float32 [128, 64, 256], P('space'), may hold values from 0.1 to 1
- dispersion: float32 [128, 64, 256], P('space'), may hold values from 0.05 to 0.3
- mobility: float32 [3, 8, 16], replicated, may hold values from -0.2 to 0.2
- material: int32 [128, 64, 256], P('space'), may hold values from 0 to 7
- fixed_mask: int32 [128, 64, 256], P('space'), may hold values 0 or 1
Outputs:
- advanced: float32 [3, 16, 128, 64, 256], P(None, 'mode', 'space')
All inputs are finite; a program needn't handle non-finite values. No bound on the sum of `fixed_mask` on one device may be relied on, other than what follows from the above.
Results may differ from a plain program's by a relative error of at most 0.0001.
Values sent between devices are 32-bit elements; how exact they have to be, the bound alone decides.
A program may use at most 128 MiB of HBM per device.

v0:
```python
import math
import jax
import jax.numpy as jnp
from jax import lax
from jax.sharding import PartitionSpec as P

STEPS = 2
TIME_STEP = 0.1
MOBILE_BASE = 0.7


def padded(array, sides, width):
    for axis, dim in sides:
        size, length = (lax.axis_size(axis), array.shape[dim])
        up = [(i, (i + 1) % size) for i in range(size - 1)]
        down = [(j, i) for i, j in up]
        last = lax.slice_in_dim(array, length - width, length, axis=dim)
        first = lax.slice_in_dim(array, 0, width, axis=dim)
        before = lax.ppermute(last, axis, up)
        after = lax.ppermute(first, axis, down)
        array = jnp.concatenate([before, array, after], axis=dim)
    return array


def legendre_weight(order):
    return math.comb(2 * order, order) / 4.0**order


def triple_table(terms_count):
    entries = []
    for degree_a in range(terms_count):
        slab_values = []
        for degree_b in range(terms_count):
            row_values = []
            for degree_c in range(terms_count):
                degree_sum = degree_a + degree_b + degree_c
                halfsum = degree_sum // 2
                amount = 0.0
                if (
                    degree_sum % 2 == 0
                    and halfsum >= degree_a
                    and (halfsum >= degree_b)
                    and (halfsum >= degree_c)
                ):
                    amount = (
                        legendre_weight(halfsum - degree_a)
                        * legendre_weight(halfsum - degree_b)
                        * legendre_weight(halfsum - degree_c)
                    )
                    amount = amount / legendre_weight(halfsum) / (degree_sum + 1)
                    amount = amount * math.sqrt(
                        (2 * degree_a + 1) * (2 * degree_b + 1) * (2 * degree_c + 1)
                    )
                row_values.append(amount)
            slab_values.append(row_values)
        entries.append(slab_values)
    return jnp.asarray(entries, jnp.float32)


def stencil(x_padded, y_padded, velocity, dispersion):
    middle = x_padded[:, :, 2:-2]
    left_two = x_padded[:, :, :-4]
    left_one = x_padded[:, :, 1:-3]
    right_one = x_padded[:, :, 3:-1]
    right_two = x_padded[:, :, 4:]
    lower_y = y_padded[:, :, :, :-2]
    upper_y = y_padded[:, :, :, 2:]
    z_padded = jnp.pad(middle, ((0, 0), (0, 0), (0, 0), (0, 0), (1, 1)))
    lower_z = z_padded[:, :, :, :, :-2]
    upper_z = z_padded[:, :, :, :, 2:]
    spread = (16.0 * (left_one + right_one) - (left_two + right_two) - 30.0 * middle) / 12.0
    spread = spread + (lower_y + upper_y) + (lower_z + upper_z) - 4.0 * middle
    carried = (2.0 * right_one + 3.0 * middle - 6.0 * left_one + left_two) / 6.0
    return dispersion[None, None] * spread - velocity[None, None] * carried


def class_terms(total, class_mats, piece, picks):

    def add_class(klass, running):
        matrix = lax.dynamic_index_in_dim(class_mats, klass, 1, keepdims=False)
        mixed = jnp.einsum("mij,mjxyz->mixyz", matrix, piece, precision=lax.Precision.HIGHEST)
        chosen = lax.dynamic_index_in_dim(picks, klass, 0, keepdims=False)
        return running + chosen[None, None] * mixed

    return lax.fori_loop(0, class_mats.shape[1], add_class, total)


def on_device(field, velocity, dispersion, mobility, material, fixed_mask):
    modes = mobility.shape[2]
    classes = mobility.shape[1]
    triple = triple_table(modes)
    class_mats = jnp.einsum("ijk,mck->mcij", triple, mobility, precision=lax.Precision.HIGHEST)
    mode_count = lax.axis_size("mode")
    mode_index = lax.axis_index("mode")
    rows_local = field.shape[3] // mode_count
    picks = (material[None] == jnp.arange(classes, dtype=jnp.int32)[:, None, None, None]).astype(
        jnp.float32
    )
    movable = (1 - fixed_mask).astype(jnp.float32)

    def rows_of(array, axis):
        return lax.dynamic_slice_in_dim(array, mode_index * rows_local, rows_local, axis)

    state = lax.all_to_all(field, "mode", split_axis=3, concat_axis=1, tiled=True)
    speed_here = rows_of(velocity, 1)
    spread_here = rows_of(dispersion, 1)
    picks_here = rows_of(picks, 2)
    movable_here = rows_of(movable, 1)
    for sweep_index in range(STEPS):
        x_padded = padded(state, (("space", 2),), 2)
        y_padded = padded(state, (("mode", 3),), 1)
        operated = stencil(x_padded, y_padded, speed_here, spread_here)
        coupled = class_terms(MOBILE_BASE * operated, class_mats, operated, picks_here)
        state = state + TIME_STEP * movable_here[None, None] * coupled
    state = lax.all_to_all(state, "mode", split_axis=1, concat_axis=3, tiled=True)
    return state


def solution(mesh):
    in_specs = (
        P(None, "mode", "space", None, None),
        P("space", None, None),
        P("space", None, None),
        P(),
        P("space", None, None),
        P("space", None, None),
    )
    out_specs = P(None, "mode", "space", None, None)
    return jax.shard_map(
        on_device, mesh=mesh, in_specs=in_specs, out_specs=out_specs, check_vma=False
    )
```

profile of v0, /device:TPU:10, one launch (start us, length us, event | category | flops | bytes accessed | tf_op | source)
XLA Modules:
  0.0 968.9 jit_solution(4053792120406774539)
XLA Ops:
  0.0 16.7 %copy.12 = f32[3,8,8,64,256]{4,2,1,0,3:T(8,128)} copy(f32[3,8,8,64,256]{4,3,2,1,0:T(8,128)} %param.11) | data formatting | bytes 25165824 | tf_op args[0]
  16.7 152.3 %all_to_all.36 = f32[3,8,8,64,256]{4,2,1,0,3:T(8,128)} all-to-all(f32[3,8,8,64,256]{4,2,1,0,3:T(8,128)} %copy.12), channel_id=1, replica_groups=mesh['space'=16,'mode'=2] {'mode'}, dimensions={3} | all-to-all | bytes 25165824 | tf_op jit(solution)/shard_map/all_to_all | solution.py:104
  169.0 16.6 %copy.13 = f32[3,2,8,8,32,256]{5,4,3,0,2,1:T(8,128)} copy(f32[3,2,8,8,32,256]{5,3,2,0,4,1:T(8,128)} %bitcast.53) | data formatting | bytes 25165824 | tf_op jit(solution)/shard_map/all_to_all | solution.py:104
  218.5 46.5 %collective-permute-done = f32[3,16,2,32,256]{4,3,2,0,1:T(8,128)} collective-permute-done((f32[3,16,2,32,256]{4,3,2,0,1:T(8,128)}, f32[3,16,2,32,256]{4,3,2,0,1:T(8,128)}, u32[]{:S(2)}, u32[]{:S(2)}) %collective-permute-start) | collective-permute-done | bytes 3145760 | tf_op jit(solution)/shard_map/ppermute | solution.py:19
  265.0 46.0 %broadcast_multiply_fusion.1 = (f32[3,16,8,32,256]{4,3,2,0,1:T(8,128)}, f32[3,16,8,32,256]{4,3,2,0,1:T(8,128)}) fusion(f32[8,32,256]{2,1,0:T(8,128)S(1)} %get-tuple-element.247, f32[3,16,8,32,256]{4,3,2,0,1:T(8,128)} %bitcast.52, f32[3,16,8,1,256]{4,3,2,0,1:T(1,128)} %collective-permute-done.3, f32[3,16,8,1,256]{4,3,2,0,1:T(1,128)} %collective-permute-done.2, ...), kind=kLoop, calls=%fused_computation.65 | loop fusion | flops 91226112 | bytes 45350912 | tf_op jit(solution)/shard_map/mul | solution.py:113
  311.0 20.3 %copy.14 = f32[3,16,8,32,256]{4,1,3,2,0:T(8,128)} copy(f32[3,16,8,32,256]{4,3,2,0,1:T(8,128)} %get-tuple-element.237) | data formatting | bytes 25165824 | tf_op jit(solution)/shard_map/while | solution.py:85
  331.3 20.4 %copy.16 = f32[3,16,8,32,256]{4,1,3,2,0:T(8,128)} copy(f32[3,16,8,32,256]{4,3,2,0,1:T(8,128)} %get-tuple-element.238) | data formatting | bytes 25165824 | tf_op jit(solution)/shard_map/while | solution.py:85
  351.6 153.1 %while.26 = (s32[]{:T(128)}, f32[3,16,8,32,256]{4,1,3,2,0:T(8,128)}, f32[8,8,32,256]{3,2,1,0:T(8,128)S(1)}, f32[3,8,16,16]{3,2,0,1:T(8,128)S(1)}, f32[3,16,8,32,256]{4,1,3,2,0:T(8,128)}, /*index=5*/s32[]{:T(128)}) while((s32[]{:T(128)}, f32[3,16,8,32,256]{4,1,3,2,0:T(8,128)}, f32[8,8,32,256]{3,2,1,0:T(8,128)S(1)}, ...), condition=%wide.region_1.2_spmd, body=%wide.region_0.1_spmd.sunk | while | flops 610271232 | bytes 38559820 | solution.py:85
  352.0 19.1 %multiply_add_fusion.4 = f32[3,16,8,32,256]{4,1,3,2,0:T(8,128)} fusion(f32[3,16,8,32,256]{4,1,3,2,0:T(8,128)} %get-tuple-element.318, f32[8,32,256]{2,1,0:T(8,128)S(1)} %dynamic-slice_bitcast_fusion.4, f32[3,16,8,32,256]{4,1,3,2,0:T(8,128)} %get-tuple-element.327, f32[3,8,16,16]{3,2,0,1:T(8,128)S(1)} %get-tuple-element.326, s32[]{:T(128)} %get-tuple-element.317), kind=kOutput, calls=%fused_computation.clone.1 | convolution fusion | flops 610271232 | bytes 38035460 | tf_op jit(solution)/shard_map/while/body/eval_jaxpr/mij,mjxyz->mixyz/dot_general | solution.py:81
  371.1 19.1 %multiply_add_fusion.4 = f32[3,16,8,32,256]{4,1,3,2,0:T(8,128)} fusion(f32[3,16,8,32,256]{4,1,3,2,0:T(8,128)} %get-tuple-element.318, f32[8,32,256]{2,1,0:T(8,128)S(1)} %dynamic-slice_bitcast_fusion.4, f32[3,16,8,32,256]{4,1,3,2,0:T(8,128)} %get-tuple-element.327, f32[3,8,16,16]{3,2,0,1:T(8,128)S(1)} %get-tuple-element.326, s32[]{:T(128)} %get-tuple-element.317), kind=kOutput, calls=%fused_computation.clone.1 | convolution fusion | flops 610271232 | bytes 38035460 | tf_op jit(solution)/shard_map/while/body/eval_jaxpr/mij,mjxyz->mixyz/dot_general | solution.py:81
  390.2 19.1 %multiply_add_fusion.4 = f32[3,16,8,32,256]{4,1,3,2,0:T(8,128)} fusion(f32[3,16,8,32,256]{4,1,3,2,0:T(8,128)} %get-tuple-element.318, f32[8,32,256]{2,1,0:T(8,128)S(1)} %dynamic-slice_bitcast_fusion.4, f32[3,16,8,32,256]{4,1,3,2,0:T(8,128)} %get-tuple-element.327, f32[3,8,16,16]{3,2,0,1:T(8,128)S(1)} %get-tuple-element.326, s32[]{:T(128)} %get-tuple-element.317), kind=kOutput, calls=%fused_computation.clone.1 | convolution fusion | flops 610271232 | bytes 38035460 | tf_op jit(solution)/shard_map/while/body/eval_jaxpr/mij,mjxyz->mixyz/dot_general | solution.py:81
  409.3 19.1 %multiply_add_fusion.4 = f32[3,16,8,32,256]{4,1,3,2,0:T(8,128)} fusion(f32[3,16,8,32,256]{4,1,3,2,0:T(8,128)} %get-tuple-element.318, f32[8,32,256]{2,1,0:T(8,128)S(1)} %dynamic-slice_bitcast_fusion.4, f32[3,16,8,32,256]{4,1,3,2,0:T(8,128)} %get-tuple-element.327, f32[3,8,16,16]{3,2,0,1:T(8,128)S(1)} %get-tuple-element.326, s32[]{:T(128)} %get-tuple-element.317), kind=kOutput, calls=%fused_computation.clone.1 | convolution fusion | flops 610271232 | bytes 38035460 | tf_op jit(solution)/shard_map/while/body/eval_jaxpr/mij,mjxyz->mixyz/dot_general | solution.py:81
  428.4 19.1 %multiply_add_fusion.4 = f32[3,16,8,32,256]{4,1,3,2,0:T(8,128)} fusion(f32[3,16,8,32,256]{4,1,3,2,0:T(8,128)} %get-tuple-element.318, f32[8,32,256]{2,1,0:T(8,128)S(1)} %dynamic-slice_bitcast_fusion.4, f32[3,16,8,32,256]{4,1,3,2,0:T(8,128)} %get-tuple-element.327, f32[3,8,16,16]{3,2,0,1:T(8,128)S(1)} %get-tuple-element.326, s32[]{:T(128)} %get-tuple-element.317), kind=kOutput, calls=%fused_computation.clone.1 | convolution fusion | flops 610271232 | bytes 38035460 | tf_op jit(solution)/shard_map/while/body/eval_jaxpr/mij,mjxyz->mixyz/dot_general | solution.py:81
  447.5 19.1 %multiply_add_fusion.4 = f32[3,16,8,32,256]{4,1,3,2,0:T(8,128)} fusion(f32[3,16,8,32,256]{4,1,3,2,0:T(8,128)} %get-tuple-element.318, f32[8,32,256]{2,1,0:T(8,128)S(1)} %dynamic-slice_bitcast_fusion.4, f32[3,16,8,32,256]{4,1,3,2,0:T(8,128)} %get-tuple-element.327, f32[3,8,16,16]{3,2,0,1:T(8,128)S(1)} %get-tuple-element.326, s32[]{:T(128)} %get-tuple-element.317), kind=kOutput, calls=%fused_computation.clone.1 | convolution fusion | flops 610271232 | bytes 38035460 | tf_op jit(solution)/shard_map/while/body/eval_jaxpr/mij,mjxyz->mixyz/dot_general | solution.py:81
  466.6 19.1 %multiply_add_fusion.4 = f32[3,16,8,32,256]{4,1,3,2,0:T(8,128)} fusion(f32[3,16,8,32,256]{4,1,3,2,0:T(8,128)} %get-tuple-element.318, f32[8,32,256]{2,1,0:T(8,128)S(1)} %dynamic-slice_bitcast_fusion.4, f32[3,16,8,32,256]{4,1,3,2,0:T(8,128)} %get-tuple-element.327, f32[3,8,16,16]{3,2,0,1:T(8,128)S(1)} %get-tuple-element.326, s32[]{:T(128)} %get-tuple-element.317), kind=kOutput, calls=%fused_computation.clone.1 | convolution fusion | flops 610271232 | bytes 38035460 | tf_op jit(solution)/shard_map/while/body/eval_jaxpr/mij,mjxyz->mixyz/dot_general | solution.py:81
  485.7 19.1 %multiply_add_fusion.4 = f32[3,16,8,32,256]{4,1,3,2,0:T(8,128)} fusion(f32[3,16,8,32,256]{4,1,3,2,0:T(8,128)} %get-tuple-element.318, f32[8,32,256]{2,1,0:T(8,128)S(1)} %dynamic-slice_bitcast_fusion.4, f32[3,16,8,32,256]{4,1,3,2,0:T(8,128)} %get-tuple-element.327, f32[3,8,16,16]{3,2,0,1:T(8,128)S(1)} %get-tuple-element.326, s32[]{:T(128)} %get-tuple-element.317), kind=kOutput, calls=%fused_computation.clone.1 | convolution fusion | flops 610271232 | bytes 38035460 | tf_op jit(solution)/shard_map/while/body/eval_jaxpr/mij,mjxyz->mixyz/dot_general | solution.py:81
  504.8 13.4 %fusion.37 = f32[3,16,8,32,256]{4,3,2,0,1:T(8,128)S(1)} fusion(f32[3,16,8,32,256]{4,1,3,2,0:T(8,128)} %get-tuple-element.193, f32[8,32,256]{2,1,0:T(8,128)S(1)} %fusion.40, f32[3,2,8,8,32,256]{5,4,3,0,2,1:T(8,128)} %copy.13), kind=kLoop, calls=%fused_computation.63 | loop fusion | flops 6291456 | bytes 38010880 | tf_op jit(solution)/shard_map/add | solution.py:114
  539.2 52.5 %collective-permute-done.4 = f32[3,16,2,32,256]{4,3,2,0,1:T(8,128)S(1)} collective-permute-done((f32[3,16,2,32,256]{4,3,2,0,1:T(8,128)S(1)}, f32[3,16,2,32,256]{4,3,2,0,1:T(8,128)S(1)}, u32[]{:S(2)}, u32[]{:S(2)}) %collective-permute-start.4) | collective-permute-done | bytes 3145760 | tf_op jit(solution)/shard_map/ppermute | solution.py:19
  593.4 45.7 %broadcast_multiply_fusion = (f32[3,16,8,32,256]{4,3,2,0,1:T(8,128)}, f32[3,16,8,32,256]{4,3,2,0,1:T(8,128)}) fusion(f32[8,32,256]{2,1,0:T(8,128)S(1)} %get-tuple-element.247, f32[3,16,8,32,256]{4,3,2,0,1:T(8,128)} %copy-done.2, f32[3,16,8,1,256]{4,3,2,0,1:T(1,128)} %copy-done.5, f32[3,16,8,1,256]{4,3,2,0,1:T(1,128)} %copy-done.4, ...), kind=kLoop, calls=%fused_computation.64 | loop fusion | flops 91226112 | bytes 45350912 | tf_op jit(solution)/shard_map/mul | solution.py:113
  639.1 20.3 %copy.18 = f32[3,16,8,32,256]{4,1,3,2,0:T(8,128)} copy(f32[3,16,8,32,256]{4,3,2,0,1:T(8,128)} %get-tuple-element.235) | data formatting | bytes 25165824 | tf_op jit(solution)/shard_map/while | solution.py:85
  659.4 20.4 %copy.20 = f32[3,16,8,32,256]{4,1,3,2,0:T(8,128)} copy(f32[3,16,8,32,256]{4,3,2,0,1:T(8,128)} %get-tuple-element.236) | data formatting | bytes 25165824 | tf_op jit(solution)/shard_map/while | solution.py:85
  679.8 153.0 %while.27 = (s32[]{:T(128)}, f32[3,16,8,32,256]{4,1,3,2,0:T(8,128)}, f32[8,8,32,256]{3,2,1,0:T(8,128)S(1)}, f32[3,8,16,16]{3,2,0,1:T(8,128)S(1)}, f32[3,16,8,32,256]{4,1,3,2,0:T(8,128)}, /*index=5*/s32[]{:T(128)}) while((s32[]{:T(128)}, f32[3,16,8,32,256]{4,1,3,2,0:T(8,128)}, f32[8,8,32,256]{3,2,1,0:T(8,128)S(1)}, ...), condition=%wide.region_3.4_spmd, body=%wide.region_2.3_spmd.sunk | while | flops 610271232 | bytes 38559820 | solution.py:85
  680.1 19.1 %multiply_add_fusion.5 = f32[3,16,8,32,256]{4,1,3,2,0:T(8,128)} fusion(f32[3,16,8,32,256]{4,1,3,2,0:T(8,128)} %get-tuple-element.336, f32[8,32,256]{2,1,0:T(8,128)S(1)} %dynamic-slice_bitcast_fusion.5, f32[3,16,8,32,256]{4,1,3,2,0:T(8,128)} %get-tuple-element.345, f32[3,8,16,16]{3,2,0,1:T(8,128)S(1)} %get-tuple-element.344, s32[]{:T(128)} %get-tuple-element.335), kind=kOutput, calls=%fused_computation.5.clone.1 | convolution fusion | flops 610271232 | bytes 38035460 | tf_op jit(solution)/shard_map/while/body/eval_jaxpr/mij,mjxyz->mixyz/dot_general | solution.py:81
  699.2 19.1 %multiply_add_fusion.5 = f32[3,16,8,32,256]{4,1,3,2,0:T(8,128)} fusion(f32[3,16,8,32,256]{4,1,3,2,0:T(8,128)} %get-tuple-element.336, f32[8,32,256]{2,1,0:T(8,128)S(1)} %dynamic-slice_bitcast_fusion.5, f32[3,16,8,32,256]{4,1,3,2,0:T(8,128)} %get-tuple-element.345, f32[3,8,16,16]{3,2,0,1:T(8,128)S(1)} %get-tuple-element.344, s32[]{:T(128)} %get-tuple-element.335), kind=kOutput, calls=%fused_computation.5.clone.1 | convolution fusion | flops 610271232 | bytes 38035460 | tf_op jit(solution)/shard_map/while/body/eval_jaxpr/mij,mjxyz->mixyz/dot_general | solution.py:81
  718.2 19.1 %multiply_add_fusion.5 = f32[3,16,8,32,256]{4,1,3,2,0:T(8,128)} fusion(f32[3,16,8,32,256]{4,1,3,2,0:T(8,128)} %get-tuple-element.336, f32[8,32,256]{2,1,0:T(8,128)S(1)} %dynamic-slice_bitcast_fusion.5, f32[3,16,8,32,256]{4,1,3,2,0:T(8,128)} %get-tuple-element.345, f32[3,8,16,16]{3,2,0,1:T(8,128)S(1)} %get-tuple-element.344, s32[]{:T(128)} %get-tuple-element.335), kind=kOutput, calls=%fused_computation.5.clone.1 | convolution fusion | flops 610271232 | bytes 38035460 | tf_op jit(solution)/shard_map/while/body/eval_jaxpr/mij,mjxyz->mixyz/dot_general | solution.py:81
  737.3 19.1 %multiply_add_fusion.5 = f32[3,16,8,32,256]{4,1,3,2,0:T(8,128)} fusion(f32[3,16,8,32,256]{4,1,3,2,0:T(8,128)} %get-tuple-element.336, f32[8,32,256]{2,1,0:T(8,128)S(1)} %dynamic-slice_bitcast_fusion.5, f32[3,16,8,32,256]{4,1,3,2,0:T(8,128)} %get-tuple-element.345, f32[3,8,16,16]{3,2,0,1:T(8,128)S(1)} %get-tuple-element.344, s32[]{:T(128)} %get-tuple-element.335), kind=kOutput, calls=%fused_computation.5.clone.1 | convolution fusion | flops 610271232 | bytes 38035460 | tf_op jit(solution)/shard_map/while/body/eval_jaxpr/mij,mjxyz->mixyz/dot_general | solution.py:81
  756.4 19.1 %multiply_add_fusion.5 = f32[3,16,8,32,256]{4,1,3,2,0:T(8,128)} fusion(f32[3,16,8,32,256]{4,1,3,2,0:T(8,128)} %get-tuple-element.336, f32[8,32,256]{2,1,0:T(8,128)S(1)} %dynamic-slice_bitcast_fusion.5, f32[3,16,8,32,256]{4,1,3,2,0:T(8,128)} %get-tuple-element.345, f32[3,8,16,16]{3,2,0,1:T(8,128)S(1)} %get-tuple-element.344, s32[]{:T(128)} %get-tuple-element.335), kind=kOutput, calls=%fused_computation.5.clone.1 | convolution fusion | flops 610271232 | bytes 38035460 | tf_op jit(solution)/shard_map/while/body/eval_jaxpr/mij,mjxyz->mixyz/dot_general | solution.py:81
  775.5 19.1 %multiply_add_fusion.5 = f32[3,16,8,32,256]{4,1,3,2,0:T(8,128)} fusion(f32[3,16,8,32,256]{4,1,3,2,0:T(8,128)} %get-tuple-element.336, f32[8,32,256]{2,1,0:T(8,128)S(1)} %dynamic-slice_bitcast_fusion.5, f32[3,16,8,32,256]{4,1,3,2,0:T(8,128)} %get-tuple-element.345, f32[3,8,16,16]{3,2,0,1:T(8,128)S(1)} %get-tuple-element.344, s32[]{:T(128)} %get-tuple-element.335), kind=kOutput, calls=%fused_computation.5.clone.1 | convolution fusion | flops 610271232 | bytes 38035460 | tf_op jit(solution)/shard_map/while/body/eval_jaxpr/mij,mjxyz->mixyz/dot_general | solution.py:81
  794.6 19.1 %multiply_add_fusion.5 = f32[3,16,8,32,256]{4,1,3,2,0:T(8,128)} fusion(f32[3,16,8,32,256]{4,1,3,2,0:T(8,128)} %get-tuple-element.336, f32[8,32,256]{2,1,0:T(8,128)S(1)} %dynamic-slice_bitcast_fusion.5, f32[3,16,8,32,256]{4,1,3,2,0:T(8,128)} %get-tuple-element.345, f32[3,8,16,16]{3,2,0,1:T(8,128)S(1)} %get-tuple-element.344, s32[]{:T(128)} %get-tuple-element.335), kind=kOutput, calls=%fused_computation.5.clone.1 | convolution fusion | flops 610271232 | bytes 38035460 | tf_op jit(solution)/shard_map/while/body/eval_jaxpr/mij,mjxyz->mixyz/dot_general | solution.py:81
  813.7 19.1 %multiply_add_fusion.5 = f32[3,16,8,32,256]{4,1,3,2,0:T(8,128)} fusion(f32[3,16,8,32,256]{4,1,3,2,0:T(8,128)} %get-tuple-element.336, f32[8,32,256]{2,1,0:T(8,128)S(1)} %dynamic-slice_bitcast_fusion.5, f32[3,16,8,32,256]{4,1,3,2,0:T(8,128)} %get-tuple-element.345, f32[3,8,16,16]{3,2,0,1:T(8,128)S(1)} %get-tuple-element.344, s32[]{:T(128)} %get-tuple-element.335), kind=kOutput, calls=%fused_computation.5.clone.1 | convolution fusion | flops 610271232 | bytes 38035460 | tf_op jit(solution)/shard_map/while/body/eval_jaxpr/mij,mjxyz->mixyz/dot_general | solution.py:81
  832.8 13.4 %fusion.36 = f32[3,16,8,32,256]{4,3,2,0,1:T(8,128)S(1)} fusion(f32[3,16,8,32,256]{4,3,2,0,1:T(8,128)} %copy-done.2, f32[3,16,8,32,256]{4,1,3,2,0:T(8,128)} %get-tuple-element.194, f32[8,32,256]{2,1,0:T(8,128)S(1)} %fusion.40), kind=kLoop, calls=%fused_computation.61 | loop fusion | flops 6291456 | bytes 38010880 | tf_op jit(solution)/shard_map/add | solution.py:114
  846.2 110.0 %all_to_all.37 = f32[3,16,8,32,256]{4,3,2,0,1:T(8,128)} all-to-all(f32[3,16,8,32,256]{4,3,2,0,1:T(8,128)S(1)} %fusion.36), channel_id=1, replica_groups=mesh['space'=16,'mode'=2] {'mode'}, dimensions={1} | all-to-all | bytes 25165824 | tf_op jit(solution)/shard_map/all_to_all | solution.py:115
  (63 shorter events, 67.8 us)
Async XLA Ops:
  0.0 199.1 %copy-start = (s32[8,64,256]{2,1,0:T(8,128)S(1)}, s32[8,64,256]{2,1,0:T(8,128)}, u32[]{:S(2)}) copy-start(s32[8,64,256]{2,1,0:T(8,128)} %param.15) | copy-start | bytes 1572868
  185.6 12.3 %copy-start.9 = (f32[16,16,16,1]{2,1,3,0:T(8,128)S(1)}, f32[16,16,16,1]{2,1,3,0:T(8,128)}, u32[]{:S(2)}) copy-start(f32[16,16,16,1]{2,1,3,0:T(8,128)} %constant.101) | copy-start | bytes 49156
  185.6 12.4 %copy-start.10 = (f32[3,8,16]{2,1,0:T(8,128)S(1)}, f32[3,8,16]{2,1,0:T(8,128)}, u32[]{:S(2)}) copy-start(f32[3,8,16]{2,1,0:T(8,128)} %param.14) | copy-start | bytes 4612
  185.6 13.5 %copy-start.7 = (f32[8,64,256]{2,1,0:T(8,128)S(1)}, f32[8,64,256]{2,1,0:T(8,128)}, u32[]{:S(2)}) copy-start(f32[8,64,256]{2,1,0:T(8,128)} %param.12) | copy-start | bytes 1572868
  185.6 13.5 %copy-start.8 = (f32[8,64,256]{2,1,0:T(8,128)S(1)}, f32[8,64,256]{2,1,0:T(8,128)}, u32[]{:S(2)}) copy-start(f32[8,64,256]{2,1,0:T(8,128)} %param.13) | copy-start | bytes 1572868
  185.6 21.5 %copy-start.6 = (s32[8,64,256]{2,1,0:T(8,128)S(1)}, s32[8,64,256]{2,1,0:T(8,128)}, u32[]{:S(2)}) copy-start(s32[8,64,256]{2,1,0:T(8,128)} %param.16) | copy-start | bytes 1572868
  192.4 72.6 %collective-permute-start = (f32[3,16,2,32,256]{4,3,2,0,1:T(8,128)}, f32[3,16,2,32,256]{4,3,2,0,1:T(8,128)}, u32[]{:S(2)}, u32[]{:S(2)}) collective-permute-start(f32[3,16,2,32,256]{4,3,2,0,1:T(8,128)} %get-tuple-element.243), channel_id=1, source_target_pairs={{0,2},{2,4},{4,6},{6,8},{8,10},{10,12},{12,14},{14,16},{16,18},{18... | collective-permute-start | bytes 9437192 | tf_op jit(solution)/shard_map/ppermute | solution.py:19
  194.3 70.7 %collective-permute-start.1 = (f32[3,16,2,32,256]{4,3,2,0,1:T(8,128)}, f32[3,16,2,32,256]{4,3,2,0,1:T(8,128)}, u32[]{:S(2)}, u32[]{:S(2)}) collective-permute-start(f32[3,16,2,32,256]{4,3,2,0,1:T(8,128)} %get-tuple-element.244), channel_id=1, source_target_pairs={{2,0},{4,2},{6,4},{8,6},{10,8},{12,10},{14,12},{16,14},{18,16},{20... | collective-permute-start | bytes 9437192 | tf_op jit(solution)/shard_map/ppermute | solution.py:20
  202.8 10.7 %collective-permute-start.2 = (f32[3,16,8,1,256]{4,3,2,0,1:T(1,128)S(1)}, f32[3,16,8,1,256]{4,3,2,0,1:T(1,128)}, u32[]{:S(2)}, u32[]{:S(2)}) collective-permute-start(f32[3,16,8,1,256]{4,3,2,0,1:T(1,128)S(1)} %get-tuple-element.245), channel_id=1, source_target_pairs={{0,1},{2,3},{4,5},{6,7},{8,9},{10,11},{12,13},{14,15},{16,17},{18,... | collective-permute-start | bytes 1179656 | tf_op jit(solution)/shard_map/ppermute | solution.py:19
  205.8 12.7 %collective-permute-start.3 = (f32[3,16,8,1,256]{4,3,2,0,1:T(1,128)S(1)}, f32[3,16,8,1,256]{4,3,2,0,1:T(1,128)}, u32[]{:S(2)}, u32[]{:S(2)}) collective-permute-start(f32[3,16,8,1,256]{4,3,2,0,1:T(1,128)S(1)} %get-tuple-element.246), channel_id=1, source_target_pairs={{1,0},{3,2},{5,4},{7,6},{9,8},{11,10},{13,12},{15,14},{17,16},{19,... | collective-permute-start | bytes 1179656 | tf_op jit(solution)/shard_map/ppermute | solution.py:20
  518.2 6.7 copy-start.2
  519.3 72.3 %collective-permute-start.4 = (f32[3,16,2,32,256]{4,3,2,0,1:T(8,128)S(1)}, f32[3,16,2,32,256]{4,3,2,0,1:T(8,128)S(1)}, u32[]{:S(2)}, u32[]{:S(2)}) collective-permute-start(f32[3,16,2,32,256]{4,3,2,0,1:T(8,128)S(1)} %get-tuple-element.239), channel_id=1, source_target_pairs={{0,2},{2,4},{4,6},{6,8},{8,10},{10,12},{12,14},{14,16},{16,18},{18... | collective-permute-start | bytes 9437192 | tf_op jit(solution)/shard_map/ppermute | solution.py:19
  521.3 72.1 %collective-permute-start.5 = (f32[3,16,2,32,256]{4,3,2,0,1:T(8,128)S(1)}, f32[3,16,2,32,256]{4,3,2,0,1:T(8,128)}, u32[]{:S(2)}, u32[]{:S(2)}) collective-permute-start(f32[3,16,2,32,256]{4,3,2,0,1:T(8,128)S(1)} %get-tuple-element.240), channel_id=1, source_target_pairs={{2,0},{4,2},{6,4},{8,6},{10,8},{12,10},{14,12},{16,14},{18,16},{20... | collective-permute-start | bytes 9437192 | tf_op jit(solution)/shard_map/ppermute | solution.py:20
  525.5 9.5 collective-permute-start.6
  527.8 11.4 %collective-permute-start.7 = (f32[3,16,8,1,256]{4,3,2,0,1:T(1,128)S(1)}, f32[3,16,8,1,256]{4,3,2,0,1:T(1,128)S(1)}, u32[]{:S(2)}, u32[]{:S(2)}) collective-permute-start(f32[3,16,8,1,256]{4,3,2,0,1:T(1,128)S(1)} %get-tuple-element.242), channel_id=1, source_target_pairs={{1,0},{3,2},{5,4},{7,6},{9,8},{11,10},{13,12},{15,14},{17,16},{19,... | collective-permute-start | bytes 1179656 | tf_op jit(solution)/shard_map/ppermute | solution.py:20
  535.0 56.6 %copy-start.4 = (f32[3,16,8,1,256]{4,3,2,0,1:T(1,128)}, f32[3,16,8,1,256]{4,3,2,0,1:T(1,128)S(1)}, u32[]{:S(2)}) copy-start(f32[3,16,8,1,256]{4,3,2,0,1:T(1,128)S(1)} %collective-permute-done.6) | copy-start | bytes 1179652
  539.2 52.5 %copy-start.5 = (f32[3,16,8,1,256]{4,3,2,0,1:T(1,128)}, f32[3,16,8,1,256]{4,3,2,0,1:T(1,128)S(1)}, u32[]{:S(2)}) copy-start(f32[3,16,8,1,256]{4,3,2,0,1:T(1,128)S(1)} %collective-permute-done.7) | copy-start | bytes 1179652
  591.6 1.7 copy-start.3
  956.3 12.2 %copy-start.1 = (s32[8,64,256]{2,1,0:T(8,128)S(1)}, s32[8,64,256]{2,1,0:T(8,128)}, u32[]{:S(2)}) copy-start(s32[8,64,256]{2,1,0:T(8,128)} %param.15) | copy-start | bytes 1572868
where the time goes:
time: 975 us; the launch traced here: 969 us
  matrix products  306 us (31%)
  blocking collectives  262 us (27%)
  local copies, waits for them, and re-layouts  141 us (14%)
  waiting for transfers between devices  120 us (12%)
  other arithmetic  119 us (12%)
  starting transfers between devices  18.9 us (2%)
    dot_general x16, matrix products, add_class(): jnp.einsum('mij,mjxyz->mixyz', matrix, piece, precision=lax.Precision.HIG...  305 us
    all_to_all x1, blocking collectives, on_device(): lax.all_to_all(field, 'mode', split_axis=3, concat_axis=1, tiled=True)  152 us
    ppermute x4, waiting for transfers between devices, padded(): before = lax.ppermute(last, axis, up)  111 us
    all_to_all x1, blocking collectives, on_device(): lax.all_to_all(state, 'mode', split_axis=1, concat_axis=3, tiled=True)  110 us
    mul x2, other arithmetic, on_device(): MOBILE_BASE * operated  91.7 us
    while x5, local copies, waits for them, and re-layouts, class_terms(): return lax.fori_loop(0, class_mats.shape[1], add_class, total)  81.4 us
    add x2, other arithmetic, on_device(): state = state + TIME_STEP * movable_here[None, None] * coupled  26.9 us
  transfers between devices with their start and end apart: 8, of which 6 were waited for; matrix products, arithmetic and copies ran while one was open for 1% of the time, Pallas kernels for 0%

commit v1 on v0

--- a/solution.py
+++ b/solution.py
@@ -3,6 +3,7 @@
 import jax.numpy as jnp
 from jax import lax
 from jax.sharding import PartitionSpec as P
+from jax.lax import all_to_all, axis_size
 
 STEPS = 2
 TIME_STEP = 0.1
@@ -112,7 +113,19 @@
         operated = stencil(x_padded, y_padded, speed_here, spread_here)
         coupled = class_terms(MOBILE_BASE * operated, class_mats, operated, picks_here)
         state = state + TIME_STEP * movable_here[None, None] * coupled
-    state = lax.all_to_all(state, "mode", split_axis=1, concat_axis=3, tiled=True)
+
+    def handle_strings(inputs):
+        return jnp.concatenate(
+            all_to_all(
+                jnp.stack(jnp.split(inputs, axis_size("mode"), 1), 0),
+                axis_name="mode",
+                split_axis=0,
+                concat_axis=0,
+            ),
+            3,
+        )
+
+    state = handle_strings(state)
     return state
 
 

time: 975 us -> 932 us (0.956)
  local copies, waits for them, and re-layouts: 141 us -> 63.9 us
  other arithmetic: 119 us -> 139 us
  blocking collectives: 262 us -> 273 us
    while x5 -> x1, local copies, waits for them, and re-layouts: 81.4 us -> 0.05 us  [class_terms(): return lax.fori_loop(0, class_mats.shape[1], add_class, total)]
    reshape x0 -> x1, local copies, waits for them, and re-layouts: none -> 13.2 us  [handle_strings(): jnp.concatenate(all_to_all(jnp.stack(jnp.split(inputs, axis_size('mode'),...]
    all_to_all x1 -> x0, local copies, waits for them, and re-layouts: 12.2 us -> none  [on_device(): lax.all_to_all(state, 'mode', split_axis=1, concat_axis=3, tiled=True)]
    another operation x0 -> x1, other arithmetic: none -> 10.8 us  [handle_strings(): jnp.stack(jnp.split(inputs, axis_size('mode'), 1), 0)]
    another operation x0 -> x1, local copies, waits for them, and re-layouts: none -> 10.5 us  [handle_strings(): jnp.stack(jnp.split(inputs, axis_size('mode'), 1), 0)]
    mul x2, other arithmetic: 91.7 us -> 102 us  [on_device(): MOBILE_BASE * operated]
    all_to_all x1, blocking collectives: 110 us -> 120 us  [handle_strings(): all_to_all(jnp.stack(jnp.split(inputs, axis_size('mode'), 1), 0), axis_na...]
  transfers between devices with their start and end apart: 8 -> 8, of which waited for: 6 -> 6; matrix products, arithmetic and copies ran while one was open for 1% -> 0% of each run, Pallas kernels for 0% -> 0%
where the time goes in v1:
time: 932 us; the launch traced here: 925 us
  matrix products  306 us (33%)
  blocking collectives  273 us (29%)
  other arithmetic  139 us (15%)
  waiting for transfers between devices  123 us (13%)
  local copies, waits for them, and re-layouts  63.9 us (7%)
  starting transfers between devices  19.1 us (2%)
    dot_general x16, matrix products, add_class(): jnp.einsum('mij,mjxyz->mixyz', matrix, piece, precision=lax.Precision.HIG...  305 us
    all_to_all x1, blocking collectives, on_device(): lax.all_to_all(field, 'mode', split_axis=3, concat_axis=1, tiled=True)  153 us
    all_to_all x1, blocking collectives, handle_strings(): all_to_all(jnp.stack(jnp.split(inputs, axis_size('mode'), 1), 0), axis_na...  120 us
    ppermute x4, waiting for transfers between devices, padded(): before = lax.ppermute(last, axis, up)  114 us
    mul x2, other arithmetic, on_device(): MOBILE_BASE * operated  102 us
    add x2, other arithmetic, on_device(): state = state + TIME_STEP * movable_here[None, None] * coupled  25.9 us
  transfers between devices with their start and end apart: 8, of which 6 were waited for; matrix products, arithmetic and copies ran while one was open for 0% of the time, Pallas kernels for 0%

profile of v1, /device:TPU:10, one launch (start us, length us, event | category | flops | bytes accessed | tf_op | source)
XLA Modules:
  0.0 924.9 jit_solution(2315235995513681073)
XLA Ops:
  0.0 16.7 %copy.12 = f32[3,8,8,64,256]{4,2,1,0,3:T(8,128)} copy(f32[3,8,8,64,256]{4,3,2,1,0:T(8,128)} %param.11) | data formatting | bytes 25165824 | tf_op args[0]
  16.7 152.6 %all_to_all.23 = f32[3,8,8,64,256]{4,2,1,0,3:T(8,128)} all-to-all(f32[3,8,8,64,256]{4,2,1,0,3:T(8,128)} %copy.12), channel_id=1, replica_groups=mesh['space'=16,'mode'=2] {'mode'}, dimensions={3} | all-to-all | bytes 25165824 | tf_op jit(solution)/shard_map/all_to_all | solution.py:105
  169.3 13.1 %copy.23 = f32[3,2,8,8,32,256]{5,2,1,4,3,0:T(8,128)} copy(f32[3,2,8,8,32,256]{5,3,2,0,4,1:T(8,128)} %bitcast.55) | data formatting | bytes 25165824 | tf_op jit(solution)/shard_map/all_to_all | solution.py:105
  182.5 6.3 fusion.44
  212.3 49.0 %collective-permute-done = f32[3,16,2,32,256]{4,1,3,2,0:T(8,128)} collective-permute-done((f32[3,16,2,32,256]{4,1,3,2,0:T(8,128)}, f32[3,16,2,32,256]{4,1,3,2,0:T(8,128)}, u32[]{:S(2)}, u32[]{:S(2)}) %collective-permute-start) | collective-permute-done | bytes 3145760 | tf_op jit(solution)/shard_map/ppermute | solution.py:20
  261.3 51.2 %broadcast_multiply_fusion.1 = (f32[3,16,8,32,256]{4,1,3,2,0:T(8,128)}, f32[3,16,8,32,256]{4,1,3,2,0:T(8,128)}) fusion(f32[8,32,256]{2,1,0:T(8,128)S(1)} %get-tuple-element.249, f32[3,16,8,32,256]{4,1,3,2,0:T(8,128)} %bitcast.59, f32[3,16,8,1,256]{4,1,3,2,0:T(8,128)} %collective-permute-done.3, f32[3,16,8,1,256]{4,1,3,2,0:T(8,128)} %collective-permute-done.2, ...), kind=kLoop, calls=%fused_computation.67 | loop fusion | flops 91226112 | bytes 45350912 | tf_op jit(solution)/shard_map/mul | solution.py:114
  312.5 152.7 %while.26 = (s32[]{:T(128)}, f32[3,16,8,32,256]{4,1,3,2,0:T(8,128)}, f32[8,8,32,256]{3,2,1,0:T(8,128)S(1)}, f32[3,8,16,16]{3,2,0,1:T(8,128)S(1)}, f32[3,16,8,32,256]{4,1,3,2,0:T(8,128)}, /*index=5*/s32[]{:T(128)}) while((s32[]{:T(128)}, f32[3,16,8,32,256]{4,1,3,2,0:T(8,128)}, f32[8,8,32,256]{3,2,1,0:T(8,128)S(1)}, ...), condition=%wide.region_1.2_spmd, body=%wide.region_0.1_spmd.sunk | while | flops 610271232 | bytes 38559820 | solution.py:86
  312.5 19.1 %multiply_add_fusion.6 = f32[3,16,8,32,256]{4,1,3,2,0:T(8,128)} fusion(f32[3,16,8,32,256]{4,1,3,2,0:T(8,128)} %get-tuple-element.320, f32[8,32,256]{2,1,0:T(8,128)S(1)} %dynamic-slice_bitcast_fusion.4, f32[3,16,8,32,256]{4,1,3,2,0:T(8,128)} %get-tuple-element.329, f32[3,8,16,16]{3,2,0,1:T(8,128)S(1)} %get-tuple-element.328, s32[]{:T(128)} %get-tuple-element.319), kind=kOutput, calls=%fused_computation.clone.1 | convolution fusion | flops 610271232 | bytes 38035460 | tf_op jit(solution)/shard_map/while/body/eval_jaxpr/mij,mjxyz->mixyz/dot_general | solution.py:82
  331.6 19.1 %multiply_add_fusion.6 = f32[3,16,8,32,256]{4,1,3,2,0:T(8,128)} fusion(f32[3,16,8,32,256]{4,1,3,2,0:T(8,128)} %get-tuple-element.320, f32[8,32,256]{2,1,0:T(8,128)S(1)} %dynamic-slice_bitcast_fusion.4, f32[3,16,8,32,256]{4,1,3,2,0:T(8,128)} %get-tuple-element.329, f32[3,8,16,16]{3,2,0,1:T(8,128)S(1)} %get-tuple-element.328, s32[]{:T(128)} %get-tuple-element.319), kind=kOutput, calls=%fused_computation.clone.1 | convolution fusion | flops 610271232 | bytes 38035460 | tf_op jit(solution)/shard_map/while/body/eval_jaxpr/mij,mjxyz->mixyz/dot_general | solution.py:82
  350.7 19.1 %multiply_add_fusion.6 = f32[3,16,8,32,256]{4,1,3,2,0:T(8,128)} fusion(f32[3,16,8,32,256]{4,1,3,2,0:T(8,128)} %get-tuple-element.320, f32[8,32,256]{2,1,0:T(8,128)S(1)} %dynamic-slice_bitcast_fusion.4, f32[3,16,8,32,256]{4,1,3,2,0:T(8,128)} %get-tuple-element.329, f32[3,8,16,16]{3,2,0,1:T(8,128)S(1)} %get-tuple-element.328, s32[]{:T(128)} %get-tuple-element.319), kind=kOutput, calls=%fused_computation.clone.1 | convolution fusion | flops 610271232 | bytes 38035460 | tf_op jit(solution)/shard_map/while/body/eval_jaxpr/mij,mjxyz->mixyz/dot_general | solution.py:82
  369.8 19.1 %multiply_add_fusion.6 = f32[3,16,8,32,256]{4,1,3,2,0:T(8,128)} fusion(f32[3,16,8,32,256]{4,1,3,2,0:T(8,128)} %get-tuple-element.320, f32[8,32,256]{2,1,0:T(8,128)S(1)} %dynamic-slice_bitcast_fusion.4, f32[3,16,8,32,256]{4,1,3,2,0:T(8,128)} %get-tuple-element.329, f32[3,8,16,16]{3,2,0,1:T(8,128)S(1)} %get-tuple-element.328, s32[]{:T(128)} %get-tuple-element.319), kind=kOutput, calls=%fused_computation.clone.1 | convolution fusion | flops 610271232 | bytes 38035460 | tf_op jit(solution)/shard_map/while/body/eval_jaxpr/mij,mjxyz->mixyz/dot_general | solution.py:82
  388.9 19.1 %multiply_add_fusion.6 = f32[3,16,8,32,256]{4,1,3,2,0:T(8,128)} fusion(f32[3,16,8,32,256]{4,1,3,2,0:T(8,128)} %get-tuple-element.320, f32[8,32,256]{2,1,0:T(8,128)S(1)} %dynamic-slice_bitcast_fusion.4, f32[3,16,8,32,256]{4,1,3,2,0:T(8,128)} %get-tuple-element.329, f32[3,8,16,16]{3,2,0,1:T(8,128)S(1)} %get-tuple-element.328, s32[]{:T(128)} %get-tuple-element.319), kind=kOutput, calls=%fused_computation.clone.1 | convolution fusion | flops 610271232 | bytes 38035460 | tf_op jit(solution)/shard_map/while/body/eval_jaxpr/mij,mjxyz->mixyz/dot_general | solution.py:82
  408.0 19.1 %multiply_add_fusion.6 = f32[3,16,8,32,256]{4,1,3,2,0:T(8,128)} fusion(f32[3,16,8,32,256]{4,1,3,2,0:T(8,128)} %get-tuple-element.320, f32[8,32,256]{2,1,0:T(8,128)S(1)} %dynamic-slice_bitcast_fusion.4, f32[3,16,8,32,256]{4,1,3,2,0:T(8,128)} %get-tuple-element.329, f32[3,8,16,16]{3,2,0,1:T(8,128)S(1)} %get-tuple-element.328, s32[]{:T(128)} %get-tuple-element.319), kind=kOutput, calls=%fused_computation.clone.1 | convolution fusion | flops 610271232 | bytes 38035460 | tf_op jit(solution)/shard_map/while/body/eval_jaxpr/mij,mjxyz->mixyz/dot_general | solution.py:82
  427.1 19.1 %multiply_add_fusion.6 = f32[3,16,8,32,256]{4,1,3,2,0:T(8,128)} fusion(f32[3,16,8,32,256]{4,1,3,2,0:T(8,128)} %get-tuple-element.320, f32[8,32,256]{2,1,0:T(8,128)S(1)} %dynamic-slice_bitcast_fusion.4, f32[3,16,8,32,256]{4,1,3,2,0:T(8,128)} %get-tuple-element.329, f32[3,8,16,16]{3,2,0,1:T(8,128)S(1)} %get-tuple-element.328, s32[]{:T(128)} %get-tuple-element.319), kind=kOutput, calls=%fused_computation.clone.1 | convolution fusion | flops 610271232 | bytes 38035460 | tf_op jit(solution)/shard_map/while/body/eval_jaxpr/mij,mjxyz->mixyz/dot_general | solution.py:82
  446.2 19.1 %multiply_add_fusion.6 = f32[3,16,8,32,256]{4,1,3,2,0:T(8,128)} fusion(f32[3,16,8,32,256]{4,1,3,2,0:T(8,128)} %get-tuple-element.320, f32[8,32,256]{2,1,0:T(8,128)S(1)} %dynamic-slice_bitcast_fusion.4, f32[3,16,8,32,256]{4,1,3,2,0:T(8,128)} %get-tuple-element.329, f32[3,8,16,16]{3,2,0,1:T(8,128)S(1)} %get-tuple-element.328, s32[]{:T(128)} %get-tuple-element.319), kind=kOutput, calls=%fused_computation.clone.1 | convolution fusion | flops 610271232 | bytes 38035460 | tf_op jit(solution)/shard_map/while/body/eval_jaxpr/mij,mjxyz->mixyz/dot_general | solution.py:82
  465.2 11.3 %multiply_add_fusion.3 = f32[3,16,8,32,256]{4,1,3,2,0:T(8,128)S(1)} fusion(f32[3,16,8,32,256]{4,1,3,2,0:T(8,128)} %get-tuple-element.193, f32[8,32,256]{2,1,0:T(8,128)S(1)} %fusion.38, f32[3,2,8,8,32,256]{5,3,2,0,4,1:T(8,128)} %bitcast.56), kind=kLoop, calls=%fused_computation.63 | loop fusion | flops 6291456 | bytes 38010880 | tf_op jit(solution)/shard_map/add | solution.py:115
  496.8 52.8 %collective-permute-done.4 = f32[3,16,2,32,256]{4,1,3,2,0:T(8,128)S(1)} collective-permute-done((f32[3,16,2,32,256]{4,1,3,2,0:T(8,128)S(1)}, f32[3,16,2,32,256]{4,1,3,2,0:T(8,128)S(1)}, u32[]{:S(2)}, u32[]{:S(2)}) %collective-permute-start.4) | collective-permute-done | bytes 3145760 | tf_op jit(solution)/shard_map/ppermute | solution.py:20
  551.3 51.0 %broadcast_multiply_fusion = (f32[3,16,8,32,256]{4,1,3,2,0:T(8,128)}, f32[3,16,8,32,256]{4,1,3,2,0:T(8,128)}) fusion(f32[8,32,256]{2,1,0:T(8,128)S(1)} %get-tuple-element.249, f32[3,16,8,32,256]{4,1,3,2,0:T(8,128)} %copy-done.2, f32[3,16,8,1,256]{4,1,3,2,0:T(8,128)} %copy-done.5, f32[3,16,8,1,256]{4,1,3,2,0:T(8,128)} %copy-done.4, ...), kind=kLoop, calls=%fused_computation.66 | loop fusion | flops 91226112 | bytes 45350912 | tf_op jit(solution)/shard_map/mul | solution.py:114
  602.3 152.9 %while.27 = (s32[]{:T(128)}, f32[3,16,8,32,256]{4,1,3,2,0:T(8,128)}, f32[8,8,32,256]{3,2,1,0:T(8,128)S(1)}, f32[3,8,16,16]{3,2,0,1:T(8,128)S(1)}, f32[3,16,8,32,256]{4,1,3,2,0:T(8,128)}, /*index=5*/s32[]{:T(128)}) while((s32[]{:T(128)}, f32[3,16,8,32,256]{4,1,3,2,0:T(8,128)}, f32[8,8,32,256]{3,2,1,0:T(8,128)S(1)}, ...), condition=%wide.region_3.4_spmd, body=%wide.region_2.3_spmd.sunk | while | flops 610271232 | bytes 38559820 | solution.py:86
  602.3 19.1 %multiply_add_fusion.7 = f32[3,16,8,32,256]{4,1,3,2,0:T(8,128)} fusion(f32[3,16,8,32,256]{4,1,3,2,0:T(8,128)} %get-tuple-element.338, f32[8,32,256]{2,1,0:T(8,128)S(1)} %dynamic-slice_bitcast_fusion.5, f32[3,16,8,32,256]{4,1,3,2,0:T(8,128)} %get-tuple-element.347, f32[3,8,16,16]{3,2,0,1:T(8,128)S(1)} %get-tuple-element.346, s32[]{:T(128)} %get-tuple-element.337), kind=kOutput, calls=%fused_computation.5.clone.1 | convolution fusion | flops 610271232 | bytes 38035460 | tf_op jit(solution)/shard_map/while/body/eval_jaxpr/mij,mjxyz->mixyz/dot_general | solution.py:82
  621.4 19.1 %multiply_add_fusion.7 = f32[3,16,8,32,256]{4,1,3,2,0:T(8,128)} fusion(f32[3,16,8,32,256]{4,1,3,2,0:T(8,128)} %get-tuple-element.338, f32[8,32,256]{2,1,0:T(8,128)S(1)} %dynamic-slice_bitcast_fusion.5, f32[3,16,8,32,256]{4,1,3,2,0:T(8,128)} %get-tuple-element.347, f32[3,8,16,16]{3,2,0,1:T(8,128)S(1)} %get-tuple-element.346, s32[]{:T(128)} %get-tuple-element.337), kind=kOutput, calls=%fused_computation.5.clone.1 | convolution fusion | flops 610271232 | bytes 38035460 | tf_op jit(solution)/shard_map/while/body/eval_jaxpr/mij,mjxyz->mixyz/dot_general | solution.py:82
  640.5 19.1 %multiply_add_fusion.7 = f32[3,16,8,32,256]{4,1,3,2,0:T(8,128)} fusion(f32[3,16,8,32,256]{4,1,3,2,0:T(8,128)} %get-tuple-element.338, f32[8,32,256]{2,1,0:T(8,128)S(1)} %dynamic-slice_bitcast_fusion.5, f32[3,16,8,32,256]{4,1,3,2,0:T(8,128)} %get-tuple-element.347, f32[3,8,16,16]{3,2,0,1:T(8,128)S(1)} %get-tuple-element.346, s32[]{:T(128)} %get-tuple-element.337), kind=kOutput, calls=%fused_computation.5.clone.1 | convolution fusion | flops 610271232 | bytes 38035460 | tf_op jit(solution)/shard_map/while/body/eval_jaxpr/mij,mjxyz->mixyz/dot_general | solution.py:82
  659.7 19.1 %multiply_add_fusion.7 = f32[3,16,8,32,256]{4,1,3,2,0:T(8,128)} fusion(f32[3,16,8,32,256]{4,1,3,2,0:T(8,128)} %get-tuple-element.338, f32[8,32,256]{2,1,0:T(8,128)S(1)} %dynamic-slice_bitcast_fusion.5, f32[3,16,8,32,256]{4,1,3,2,0:T(8,128)} %get-tuple-element.347, f32[3,8,16,16]{3,2,0,1:T(8,128)S(1)} %get-tuple-element.346, s32[]{:T(128)} %get-tuple-element.337), kind=kOutput, calls=%fused_computation.5.clone.1 | convolution fusion | flops 610271232 | bytes 38035460 | tf_op jit(solution)/shard_map/while/body/eval_jaxpr/mij,mjxyz->mixyz/dot_general | solution.py:82
  678.8 19.1 %multiply_add_fusion.7 = f32[3,16,8,32,256]{4,1,3,2,0:T(8,128)} fusion(f32[3,16,8,32,256]{4,1,3,2,0:T(8,128)} %get-tuple-element.338, f32[8,32,256]{2,1,0:T(8,128)S(1)} %dynamic-slice_bitcast_fusion.5, f32[3,16,8,32,256]{4,1,3,2,0:T(8,128)} %get-tuple-element.347, f32[3,8,16,16]{3,2,0,1:T(8,128)S(1)} %get-tuple-element.346, s32[]{:T(128)} %get-tuple-element.337), kind=kOutput, calls=%fused_computation.5.clone.1 | convolution fusion | flops 610271232 | bytes 38035460 | tf_op jit(solution)/shard_map/while/body/eval_jaxpr/mij,mjxyz->mixyz/dot_general | solution.py:82
  697.9 19.1 %multiply_add_fusion.7 = f32[3,16,8,32,256]{4,1,3,2,0:T(8,128)} fusion(f32[3,16,8,32,256]{4,1,3,2,0:T(8,128)} %get-tuple-element.338, f32[8,32,256]{2,1,0:T(8,128)S(1)} %dynamic-slice_bitcast_fusion.5, f32[3,16,8,32,256]{4,1,3,2,0:T(8,128)} %get-tuple-element.347, f32[3,8,16,16]{3,2,0,1:T(8,128)S(1)} %get-tuple-element.346, s32[]{:T(128)} %get-tuple-element.337), kind=kOutput, calls=%fused_computation.5.clone.1 | convolution fusion | flops 610271232 | bytes 38035460 | tf_op jit(solution)/shard_map/while/body/eval_jaxpr/mij,mjxyz->mixyz/dot_general | solution.py:82
  717.0 19.1 %multiply_add_fusion.7 = f32[3,16,8,32,256]{4,1,3,2,0:T(8,128)} fusion(f32[3,16,8,32,256]{4,1,3,2,0:T(8,128)} %get-tuple-element.338, f32[8,32,256]{2,1,0:T(8,128)S(1)} %dynamic-slice_bitcast_fusion.5, f32[3,16,8,32,256]{4,1,3,2,0:T(8,128)} %get-tuple-element.347, f32[3,8,16,16]{3,2,0,1:T(8,128)S(1)} %get-tuple-element.346, s32[]{:T(128)} %get-tuple-element.337), kind=kOutput, calls=%fused_computation.5.clone.1 | convolution fusion | flops 610271232 | bytes 38035460 | tf_op jit(solution)/shard_map/while/body/eval_jaxpr/mij,mjxyz->mixyz/dot_general | solution.py:82
  736.1 19.1 %multiply_add_fusion.7 = f32[3,16,8,32,256]{4,1,3,2,0:T(8,128)} fusion(f32[3,16,8,32,256]{4,1,3,2,0:T(8,128)} %get-tuple-element.338, f32[8,32,256]{2,1,0:T(8,128)S(1)} %dynamic-slice_bitcast_fusion.5, f32[3,16,8,32,256]{4,1,3,2,0:T(8,128)} %get-tuple-element.347, f32[3,8,16,16]{3,2,0,1:T(8,128)S(1)} %get-tuple-element.346, s32[]{:T(128)} %get-tuple-element.337), kind=kOutput, calls=%fused_computation.5.clone.1 | convolution fusion | flops 610271232 | bytes 38035460 | tf_op jit(solution)/shard_map/while/body/eval_jaxpr/mij,mjxyz->mixyz/dot_general | solution.py:82
  755.2 14.6 %multiply_add_fusion.2 = f32[3,16,8,32,256]{4,1,3,2,0:T(8,128)} fusion(f32[3,16,8,32,256]{4,1,3,2,0:T(8,128)} %copy-done.2, f32[3,16,8,32,256]{4,1,3,2,0:T(8,128)} %get-tuple-element.194, f32[8,32,256]{2,1,0:T(8,128)S(1)} %fusion.38), kind=kLoop, calls=%fused_computation.62 | loop fusion | flops 6291456 | bytes 38010880 | tf_op jit(solution)/shard_map/add | solution.py:115
  769.8 10.5 %slice_bitcast_fusion.1 = (f32[1,3,8,8,32,256]{5,2,4,3,1,0:T(8,128)}, f32[1,3,8,8,32,256]{5,2,4,3,1,0:T(8,128)}) fusion(f32[3,16,8,32,256]{4,1,3,2,0:T(8,128)} %multiply_add_fusion.2), kind=kLoop, calls=%fused_computation.65 | loop fusion | bytes 25165824 | tf_op jit(solution)/shard_map/stack | solution.py:120
  780.4 10.8 %pad_maximum_fusion.8 = f32[2,3,8,8,32,256]{5,2,4,3,1,0:T(8,128)} fusion(f32[1,3,8,8,32,256]{5,2,4,3,1,0:T(8,128)} %get-tuple-element.240, f32[1,3,8,8,32,256]{5,2,4,3,1,0:T(8,128)} %get-tuple-element.239), kind=kLoop, calls=%fused_computation.60 | loop fusion | flops 3145728 | bytes 25165824 | tf_op jit(solution)/shard_map/stack | solution.py:120
  791.2 120.1 %all_to_all.24 = f32[2,3,8,8,32,256]{5,2,4,3,1,0:T(8,128)} all-to-all(f32[2,3,8,8,32,256]{5,2,4,3,1,0:T(8,128)} %pad_maximum_fusion.8), channel_id=1, replica_groups=mesh['space'=16,'mode'=2] {'mode'}, dimensions={0} | all-to-all | bytes 25165824 | tf_op jit(solution)/shard_map/all_to_all | solution.py:119
  911.2 13.2 %copy.16 = f32[3,8,8,2,32,256]{5,4,3,2,1,0:T(8,128)} copy(f32[3,8,8,2,32,256]{5,1,4,2,0,3:T(8,128)} %bitcast.60) | data formatting | bytes 25165824 | tf_op jit(solution)/shard_map/reshape | solution.py:118
  (61 shorter events, 45.8 us)
Async XLA Ops:
  0.0 195.4 %copy-start = (s32[8,64,256]{2,1,0:T(8,128)S(1)}, s32[8,64,256]{2,1,0:T(8,128)}, u32[]{:S(2)}) copy-start(s32[8,64,256]{2,1,0:T(8,128)} %param.15) | copy-start | bytes 1572868
  182.4 11.9 %copy-start.9 = (f32[16,16,16,1]{2,1,3,0:T(8,128)S(1)}, f32[16,16,16,1]{2,1,3,0:T(8,128)}, u32[]{:S(2)}) copy-start(f32[16,16,16,1]{2,1,3,0:T(8,128)} %constant.101) | copy-start | bytes 49156
  182.4 11.9 %copy-start.10 = (f32[3,8,16]{2,1,0:T(8,128)S(1)}, f32[3,8,16]{2,1,0:T(8,128)}, u32[]{:S(2)}) copy-start(f32[3,8,16]{2,1,0:T(8,128)} %param.14) | copy-start | bytes 4612
  182.4 13.0 %copy-start.7 = (f32[8,64,256]{2,1,0:T(8,128)S(1)}, f32[8,64,256]{2,1,0:T(8,128)}, u32[]{:S(2)}) copy-start(f32[8,64,256]{2,1,0:T(8,128)} %param.12) | copy-start | bytes 1572868
  182.4 13.0 %copy-start.8 = (f32[8,64,256]{2,1,0:T(8,128)S(1)}, f32[8,64,256]{2,1,0:T(8,128)}, u32[]{:S(2)}) copy-start(f32[8,64,256]{2,1,0:T(8,128)} %param.13) | copy-start | bytes 1572868
  182.4 18.5 %copy-start.6 = (s32[8,64,256]{2,1,0:T(8,128)S(1)}, s32[8,64,256]{2,1,0:T(8,128)}, u32[]{:S(2)}) copy-start(s32[8,64,256]{2,1,0:T(8,128)} %param.16) | copy-start | bytes 1572868
  188.7 72.6 %collective-permute-start = (f32[3,16,2,32,256]{4,1,3,2,0:T(8,128)}, f32[3,16,2,32,256]{4,1,3,2,0:T(8,128)}, u32[]{:S(2)}, u32[]{:S(2)}) collective-permute-start(f32[3,16,2,32,256]{4,1,3,2,0:T(8,128)} %get-tuple-element.245), channel_id=1, source_target_pairs={{0,2},{2,4},{4,6},{6,8},{8,10},{10,12},{12,14},{14,16},{16,18},{18... | collective-permute-start | bytes 9437192 | tf_op jit(solution)/shard_map/ppermute | solution.py:20
  190.6 70.7 %collective-permute-start.1 = (f32[3,16,2,32,256]{4,1,3,2,0:T(8,128)}, f32[3,16,2,32,256]{4,1,3,2,0:T(8,128)}, u32[]{:S(2)}, u32[]{:S(2)}) collective-permute-start(f32[3,16,2,32,256]{4,1,3,2,0:T(8,128)} %get-tuple-element.246), channel_id=1, source_target_pairs={{2,0},{4,2},{6,4},{8,6},{10,8},{12,10},{14,12},{16,14},{18,16},{20... | collective-permute-start | bytes 9437192 | tf_op jit(solution)/shard_map/ppermute | solution.py:21
  196.7 10.7 %collective-permute-start.2 = (f32[3,16,8,1,256]{4,1,3,2,0:T(8,128)S(1)}, f32[3,16,8,1,256]{4,1,3,2,0:T(8,128)}, u32[]{:S(2)}, u32[]{:S(2)}) collective-permute-start(f32[3,16,8,1,256]{4,1,3,2,0:T(8,128)S(1)} %get-tuple-element.247), channel_id=1, source_target_pairs={{0,1},{2,3},{4,5},{6,7},{8,9},{10,11},{12,13},{14,15},{16,17},{18,... | collective-permute-start | bytes 1179656 | tf_op jit(solution)/shard_map/ppermute | solution.py:20
  199.7 12.7 %collective-permute-start.3 = (f32[3,16,8,1,256]{4,1,3,2,0:T(8,128)S(1)}, f32[3,16,8,1,256]{4,1,3,2,0:T(8,128)}, u32[]{:S(2)}, u32[]{:S(2)}) collective-permute-start(f32[3,16,8,1,256]{4,1,3,2,0:T(8,128)S(1)} %get-tuple-element.248), channel_id=1, source_target_pairs={{1,0},{3,2},{5,4},{7,6},{9,8},{11,10},{13,12},{15,14},{17,16},{19,... | collective-permute-start | bytes 1179656 | tf_op jit(solution)/shard_map/ppermute | solution.py:21
  476.5 6.6 copy-start.2
  477.3 72.3 %collective-permute-start.4 = (f32[3,16,2,32,256]{4,1,3,2,0:T(8,128)S(1)}, f32[3,16,2,32,256]{4,1,3,2,0:T(8,128)S(1)}, u32[]{:S(2)}, u32[]{:S(2)}) collective-permute-start(f32[3,16,2,32,256]{4,1,3,2,0:T(8,128)S(1)} %get-tuple-element.241), channel_id=1, source_target_pairs={{0,2},{2,4},{4,6},{6,8},{8,10},{10,12},{12,14},{14,16},{16,18},{18... | collective-permute-start | bytes 9437192 | tf_op jit(solution)/shard_map/ppermute | solution.py:20
  479.4 71.9 %collective-permute-start.5 = (f32[3,16,2,32,256]{4,1,3,2,0:T(8,128)S(1)}, f32[3,16,2,32,256]{4,1,3,2,0:T(8,128)}, u32[]{:S(2)}, u32[]{:S(2)}) collective-permute-start(f32[3,16,2,32,256]{4,1,3,2,0:T(8,128)S(1)} %get-tuple-element.242), channel_id=1, source_target_pairs={{2,0},{4,2},{6,4},{8,6},{10,8},{12,10},{14,12},{16,14},{18,16},{20... | collective-permute-start | bytes 9437192 | tf_op jit(solution)/shard_map/ppermute | solution.py:21
  483.1 9.5 %collective-permute-start.6 = (f32[3,16,8,1,256]{4,1,3,2,0:T(8,128)S(1)}, f32[3,16,8,1,256]{4,1,3,2,0:T(8,128)S(1)}, u32[]{:S(2)}, u32[]{:S(2)}) collective-permute-start(f32[3,16,8,1,256]{4,1,3,2,0:T(8,128)S(1)} %get-tuple-element.243), channel_id=1, source_target_pairs={{0,1},{2,3},{4,5},{6,7},{8,9},{10,11},{12,13},{14,15},{16,17},{18,... | collective-permute-start | bytes 1179656 | tf_op jit(solution)/shard_map/ppermute | solution.py:20
  485.4 11.4 %collective-permute-start.7 = (f32[3,16,8,1,256]{4,1,3,2,0:T(8,128)S(1)}, f32[3,16,8,1,256]{4,1,3,2,0:T(8,128)S(1)}, u32[]{:S(2)}, u32[]{:S(2)}) collective-permute-start(f32[3,16,8,1,256]{4,1,3,2,0:T(8,128)S(1)} %get-tuple-element.244), channel_id=1, source_target_pairs={{1,0},{3,2},{5,4},{7,6},{9,8},{11,10},{13,12},{15,14},{17,16},{19,... | collective-permute-start | bytes 1179656 | tf_op jit(solution)/shard_map/ppermute | solution.py:21
  492.7 56.9 %copy-start.4 = (f32[3,16,8,1,256]{4,1,3,2,0:T(8,128)}, f32[3,16,8,1,256]{4,1,3,2,0:T(8,128)S(1)}, u32[]{:S(2)}) copy-start(f32[3,16,8,1,256]{4,1,3,2,0:T(8,128)S(1)} %collective-permute-done.6) | copy-start | bytes 1179652
  496.8 52.8 %copy-start.5 = (f32[3,16,8,1,256]{4,1,3,2,0:T(8,128)}, f32[3,16,8,1,256]{4,1,3,2,0:T(8,128)S(1)}, u32[]{:S(2)}) copy-start(f32[3,16,8,1,256]{4,1,3,2,0:T(8,128)S(1)} %collective-permute-done.7) | copy-start | bytes 1179652
  549.6 1.7 copy-start.3
  911.2 13.2 %copy-start.1 = (s32[8,64,256]{2,1,0:T(8,128)S(1)}, s32[8,64,256]{2,1,0:T(8,128)}, u32[]{:S(2)}) copy-start(s32[8,64,256]{2,1,0:T(8,128)} %param.15) | copy-start | bytes 1572868
